TPU v7x, 1024 devices: a whole 8x8x8 slice. The times are simulated.
1024 devices in a mesh: dp: 128 (over y_lo, z, x), mp: 8 (over y_hi, core).
Axes of the slice: x: 8, y: 8 (y_hi: 4, y_lo: 2; y = y_hi * 2 + y_lo), z: 8, core: 2. Of those that a mesh axis runs over, the one named last changes fastest.
Arguments:
- query_states: bfloat16 [16384, 8192], P('dp', 'mp'), may hold values from -35.35534 to 35.35534
- key_states: bfloat16 [16384, 1024], P('dp', 'mp'), may hold values from -3 to 3
- value_states: bfloat16 [16384, 1024], P('dp', 'mp'), may hold values from -6 to 6
- grad_context: bfloat16 [16384, 8192], P('dp', 'mp'), may hold values from -6 to 6
- inputs_normed: bfloat16 [16384, 4096], P('dp'), may hold values from -24 to 24
- projections: bfloat16 [2, 4096, 1024], P(None, None, 'mp'), may hold values from -0.09375 to 0.09375
Outputs:
- grad_query: bfloat16 [16384, 8192], P('dp', 'mp')
- grad_input: bfloat16 [16384, 4096], P('dp', 'mp')
- grad_weights: float32 [4096, 1024], P('dp', 'mp')
All inputs are finite; a program needn't handle non-finite values.
Results may differ from a plain program's by a relative error of at most 0.013.
Values may be sent and summed in bfloat16 or wider, within the bound.
A program may use at most 32 MiB of HBM per device.

v0:
```python
import math

import jax
import jax.numpy as jnp
from jax import lax
from jax.sharding import Mesh
from jax.sharding import PartitionSpec as P

HEAD_SIZE = 128
DP = ("dp_0", "dp_1", "dp_2")


def sum_in_order(blocks, axes, order):
    inside = blocks.shape[1:]
    blocks = blocks.reshape(*(lax.axis_size(a) for a in axes), *inside)
    blocks = jnp.moveaxis(blocks, order, range(len(axes))).reshape(-1, *inside)
    for k in order:
        blocks = lax.psum_scatter(blocks, axes[k], scatter_dimension=0, tiled=True)
    return blocks[0]


def cut_along(value, dim, length):
    shape = value.shape
    blocks = value.reshape(*shape[:dim], length, shape[dim] // length, *shape[dim + 1 :])
    return jnp.moveaxis(blocks, dim, 0)


def summed_rows(value, axes, order, dim):
    length = lax.axis_size(axes)
    return sum_in_order(cut_along(value, dim, length), axes, order)


def sent_and_summed(value, axis, dim):
    length = lax.axis_size(axis)
    blocks = lax.all_to_all(cut_along(value, dim, length), axis, 0, 0, tiled=True)
    return jnp.sum(blocks.astype(jnp.float32), axis=0)


def attention_grads(query_states, key_states, value_states, grad_context):
    length = query_states.shape[0]
    kv_heads = key_states.shape[1] // HEAD_SIZE
    per_group = query_states.shape[1] // key_states.shape[1]
    scale = 1.0 / math.sqrt(HEAD_SIZE)
    query_per_head = query_states.reshape(length, kv_heads, per_group, HEAD_SIZE)
    key_per_head = key_states.reshape(length, kv_heads, HEAD_SIZE)
    value_per_head = value_states.reshape(length, kv_heads, HEAD_SIZE)
    gradient_per_head = grad_context.reshape(length, kv_heads, per_group, HEAD_SIZE)
    scores = (
        jnp.einsum(
            "ikgd,jkd->kgij", query_per_head, key_per_head, preferred_element_type=jnp.float32
        )
        * scale
    )
    positions = lax.broadcasted_iota(jnp.int32, (length, length), 0)
    targets = lax.broadcasted_iota(jnp.int32, (length, length), 1)
    allowed = targets <= positions
    masked = jnp.where(allowed, scores, -1e30)
    row_max = jnp.max(masked, axis=-1, keepdims=True)
    raw_weights = jnp.where(allowed, jnp.exp(masked - row_max), 0.0)
    probs = raw_weights / jnp.sum(raw_weights, axis=-1, keepdims=True)
    probs_b = probs.astype(jnp.bfloat16)
    grad_value = jnp.einsum(
        "kgij,ikgd->jkd", probs_b, gradient_per_head, preferred_element_type=jnp.float32
    ).astype(jnp.bfloat16)
    grad_probs = jnp.einsum(
        "ikgd,jkd->kgij", gradient_per_head, value_per_head, preferred_element_type=jnp.float32
    )
    delta = jnp.sum(probs * grad_probs, axis=-1, keepdims=True)
    grad_scores = (probs * (grad_probs - delta)).astype(jnp.bfloat16)
    grad_query = (
        jnp.einsum("kgij,jkd->ikgd", grad_scores, key_per_head, preferred_element_type=jnp.float32)
        * scale
    ).astype(jnp.bfloat16)
    grad_key = (
        jnp.einsum(
            "kgij,ikgd->jkd", grad_scores, query_per_head, preferred_element_type=jnp.float32
        )
        * scale
    ).astype(jnp.bfloat16)
    return (
        grad_query.reshape(length, query_states.shape[1]),
        grad_key.reshape(length, key_states.shape[1]),
        grad_value.reshape(length, key_states.shape[1]),
    )


def body(query_states, key_states, value_states, grad_context, inputs_normed, projections):
    grad_query, grad_key, grad_value = attention_grads(
        query_states, key_states, value_states, grad_context
    )
    both_grads = jnp.stack([grad_key, grad_value])
    weight_terms = jnp.einsum(
        "sd,sc->dc", inputs_normed, grad_key, preferred_element_type=jnp.float32
    )
    summed = summed_rows(weight_terms, DP, (1, 2, 0), 0)
    grad_weights = summed / lax.axis_size(DP)
    partial_terms = jnp.einsum(
        "tsc,tdc->sd", both_grads, projections, preferred_element_type=jnp.float32
    )
    rounded_terms = partial_terms.astype(jnp.bfloat16)
    grad_input = sent_and_summed(rounded_terms, "mp", 1).astype(jnp.bfloat16)
    return (grad_query, grad_input, grad_weights)


def solution(mesh):
    torus = Mesh(mesh.devices.reshape(2, 8, 8, mesh.shape["mp"]), ("dp_0", "dp_1", "dp_2", "mp"))
    return jax.shard_map(
        body,
        mesh=torus,
        in_specs=(
            P(DP, "mp"),
            P(DP, "mp"),
            P(DP, "mp"),
            P(DP, "mp"),
            P(DP, None),
            P(None, None, "mp"),
        ),
        out_specs=(P(DP, "mp"), P(DP, "mp"), P(DP, "mp")),
        check_vma=False,
    )
```

profile of v0, /device:TPU:1, one launch (start us, length us, event | category | flops | bytes accessed | tf_op | source)
XLA Modules:
  0.0 155.2 jit_solution(1999775848160192020)
XLA Ops:
  7.2 0.0 copy-start
  7.2 0.0 reduce-scatter.4.cloned.1.call-start
  7.2 1.3 fusion.29
  8.6 0.1 fusion.9
  8.7 0.0 copy-start.3
  8.7 0.0 copy-start.1
  8.7 1.3 multiply_reduce_fusion
  10.1 0.2 fusion.10
  10.2 0.0 copy-start.2
  10.2 0.7 copy-done.2
  10.9 0.2 fusion.6
  11.2 1.8 %convolution_bitcast_fusion = f32[4096,128]{0,1:T(8,128)} fusion(bf16[128,128]{1,0:T(8,128)(2,1)S(1)} %fusion.6, bf16[128,4096]{1,0:T(8,128)(2,1)S(1)} %copy-done.1), kind=kOutput, calls=%fused_computation | convolution fusion | flops 134217728 | bytes 3178496 | tf_op jit(solution)/shard_map/sd,sc->dc/dot_general | solution.py:92
  13.0 2.9 %copy.41 = f32[4096,128]{1,0:T(8,128)} copy(f32[4096,128]{0,1:T(8,128)} %convolution_bitcast_fusion) | data formatting | bytes 4194304 | tf_op jit(solution)/shard_map/sd,sc->dc/dot_general | solution.py:92
  15.9 3.2 %copy.42 = f32[8,8,2,32,128]{4,3,2,1,0:T(8,128)} copy(f32[8,8,2,32,128]{4,3,1,0,2:T(8,128)} %bitcast.115) | data formatting | bytes 4194304 | tf_op jit(solution)/shard_map/transpose | solution.py:16
  19.1 0.0 reduce-scatter.4.cloned.1.call-update
  19.1 0.9 copy-done.5
  20.0 0.3 fusion.7
  20.3 0.8 fusion
  21.1 0.0 copy-start.4
  21.1 1.1 copy.71
  22.2 17.6 %all-to-all-start = ((bf16[8,128,512]{2,1,0:T(8,128)(2,1)}), bf16[8,128,512]{2,1,0:T(8,128)(2,1)S(1)}, u32[]{:S(2)}, u32[]{:S(2)}) async-start(bf16[8,128,512]{2,1,0:T(8,128)(2,1)} %bitcast.117), calls=%async_computation | async-start | bytes 2097152 | tf_op jit(solution)/shard_map/all_to_all | solution.py:35
  39.8 37.0 %reduce-scatter.4.cloned.1.call-done = f32[16,32,128]{2,1,0:T(8,128)} async-done(((f32[128,32,128]{2,1,0:T(8,128)}), f32[16,32,128]{2,1,0:T(8,128)}) %reduce-scatter.4.cloned.1.call-update) | async-done | bytes 262160 | tf_op jit(solution)/shard_map/reduce_scatter | solution.py:18
  76.8 0.0 reduce-scatter.6.cloned.1.call-update
  76.8 0.0 reduce-scatter.8.cloned.1.call-start
  76.8 42.0 %reduce-scatter.6.cloned.1.call-done = f32[2,32,128]{2,1,0:T(8,128)} async-done(((f32[16,32,128]{2,1,0:T(8,128)}), f32[2,32,128]{2,1,0:T(8,128)}) %reduce-scatter.6.cloned.1.call-update) | async-done | bytes 32784 | tf_op jit(solution)/shard_map/reduce_scatter | solution.py:18
  118.8 0.0 reduce-scatter.8.cloned.1.call-update
  118.8 1.2 fusion.2
  120.1 0.9 copy.43
  120.9 0.0 all-to-all-done
  120.9 0.8 reduce_sum.32
  121.7 25.6 %reduce-scatter.8.cloned.1.call-done = f32[1,32,128]{2,1,0:T(8,128)} async-done(((f32[2,32,128]{2,1,0:T(8,128)}), f32[1,32,128]{2,1,0:T(8,128)}) %reduce-scatter.8.cloned.1.call-update) | async-done | bytes 16400 | tf_op jit(solution)/shard_map/reduce_scatter | solution.py:18
  147.3 1.3 multiply_bitcast_fusion
  (7 shorter events, 0.0 us)
Async XLA Ops:
  7.2 13.1 %copy-start = (bf16[2,4096,128]{2,1,0:T(8,128)(2,1)S(1)}, bf16[2,4096,128]{2,1,0:T(8,128)(2,1)}, u32[]{:S(2)}) copy-start(bf16[2,4096,128]{2,1,0:T(8,128)(2,1)} %param.11) | copy-start | bytes 6291460
  7.2 69.6 %reduce-scatter.4.cloned.1.call-start = ((), (), s32[]{:S(2)}) async-start(), calls=%async_computation.4 | async-start | bytes 2359296 | tf_op jit(solution)/shard_map/reduce_scatter | solution.py:18
  8.7 2.2 %copy-start.3 = (bf16[128,1024]{1,0:T(8,128)(2,1)S(1)}, bf16[128,1024]{1,0:T(8,128)(2,1)}, u32[]{:S(2)}) copy-start(bf16[128,1024]{1,0:T(8,128)(2,1)} %param.6) | copy-start | bytes 786436
  8.7 2.4 %copy-start.1 = (bf16[128,4096]{1,0:T(8,128)(2,1)S(1)}, bf16[128,4096]{1,0:T(8,128)(2,1)}, u32[]{:S(2)}) copy-start(bf16[128,4096]{1,0:T(8,128)(2,1)} %param.10) | copy-start | bytes 3145732
  10.2 0.7 copy-start.2
  19.1 0.9 copy-start.5
  21.1 97.7 %copy-start.4 = (bf16[128,128]{1,0:T(8,128)(2,1)S(1)}, bf16[128,128]{1,0:T(8,128)(2,1)}, u32[]{:S(2)}) copy-start(bf16[128,128]{1,0:T(8,128)(2,1)} %param.7) | copy-start | bytes 98308
  22.2 98.7 %all-to-all-start = ((bf16[8,128,512]{2,1,0:T(8,128)(2,1)}), bf16[8,128,512]{2,1,0:T(8,128)(2,1)S(1)}, u32[]{:S(2)}, u32[]{:S(2)}) async-start(bf16[8,128,512]{2,1,0:T(8,128)(2,1)} %bitcast.117), calls=%async_computation | async-start | bytes 2097152 | tf_op jit(solution)/shard_map/all_to_all | solution.py:35
  39.8 79.1 %reduce-scatter.6.cloned.1.call-start = ((), (), s32[]{:S(2)}) async-start(), calls=%async_computation.5 | async-start | bytes 294912 | tf_op jit(solution)/shard_map/reduce_scatter | solution.py:18
  76.8 70.5 %reduce-scatter.8.cloned.1.call-start = ((), (), s32[]{:S(2)}) async-start(), calls=%async_computation.6 | async-start | bytes 49152 | tf_op jit(solution)/shard_map/reduce_scatter | solution.py:18
Sparse Core Ops, SparseCore 0:
  19.2 57.5 reduce-scatter.3
  80.1 38.6 reduce-scatter.5
  122.1 25.1 reduce-scatter.7
where the time goes:
time: 157 us; the launch traced here: 155 us
  waiting for transfers between devices  105 us (67%)
  starting transfers between devices  17.6 us (11%)
  between operations  13.9 us (9%)
  local copies, waits for them, and re-layouts  9.66 us (6%)
  matrix products  6.97 us (4%)
  other arithmetic  2.41 us (2%)
    reduce_scatter x3, waiting for transfers between devices, sum_in_order(): blocks = lax.psum_scatter(blocks, axes[k], scatter_dimension=0, tiled=True)  105 us
    all_to_all x1, starting transfers between devices, sent_and_summed(): lax.all_to_all(cut_along(value, dim, length), axis, 0, 0, tiled=True)  17.6 us
    transpose x1, local copies, waits for them, and re-layouts, sum_in_order(): blocks = jnp.moveaxis(blocks, order, range(len(axes))).reshape(-1, *inside)  3.19 us
  transfers between devices with their start and end apart: 4, of which 3 were waited for; matrix products, arithmetic and copies ran while one was open for 3% of the time, Pallas kernels for 0%

commit v1 on v0

v1 whole, which is shorter than its diff:
```python
import math

import jax
import jax.numpy as jnp
from jax import lax
from jax.experimental import pallas as pl
from jax.experimental.pallas import tpu as pltpu
from jax.sharding import Mesh
from jax.sharding import PartitionSpec as P

MESH = pl.DeviceIdType.MESH
H = 128
DP = ("yl", "z", "x")
MP = ("yh", "c")
F32 = jnp.float32
BF16 = jnp.bfloat16


def nt(a, b):
    return lax.dot_general(a, b, (((1,), (1,)), ((), ())), preferred_element_type=F32)


def tn(a, b):
    return lax.dot_general(a, b, (((0,), (0,)), ((), ())), preferred_element_type=F32)


def kernel(
    q_hbm, k_hbm, v_hbm, g_hbm, xn_hbm, pr_hbm,
    gq_hbm, gi_ref, gw_ref,
    q, k, v, g, xn, pr, pt, dst, gq, both,
    wf, mp_, mm_, rp, rm, s2, r2,
    bpo, bps, bpr, ysend_p, ysend_m, yr_p, yr_m,
    lsem, osem, xs, xr, s2s, s2r, cs, cr, ys, yr,
):
    yl = lax.axis_index("yl")
    z = lax.axis_index("z")
    x = lax.axis_index("x")
    yh = lax.axis_index("yh")
    c = lax.axis_index("c")
    nheads = q.shape[1] // H
    scale = 1.0 / math.sqrt(H)

    loads = [
        pltpu.make_async_copy(src, dst_, lsem.at[n])
        for n, (src, dst_) in enumerate(
            [(k_hbm, k), (q_hbm, q), (v_hbm, v), (g_hbm, g), (xn_hbm, xn), (pr_hbm, pr)]
        )
    ]
    for cp in loads:
        cp.start()

    a = x + c * (z - x)

    def along_a(step):
        return {"x": (x + (1 - c) * step + 8) % 8, "z": (z + c * step + 8) % 8}

    def along_b(step, ystep):
        return {
            "x": (x + c * step) % 8,
            "z": (z + (1 - c) * step) % 8,
            "yl": (yl + ystep) % 2,
        }

    def along_y(step):
        return {"yh": (yh + step + 4) % 4}

    partner = {"c": 1 - c}
    peers = [partner, along_y(1), along_y(-1), along_a(1), along_a(-1)]
    peers += [along_b(n % 8, n // 8) for n in range(1, 16)]
    barrier = pltpu.get_barrier_semaphore()
    for peer in peers:
        pl.semaphore_signal(barrier, inc=1, device_id=peer, device_id_type=MESH)

    jpos = lax.broadcasted_iota(jnp.int32, (H, H), 0)
    ipos = lax.broadcasted_iota(jnp.int32, (H, H), 1)
    allowed = jpos <= ipos
    for n in range(4):
        loads[n].wait()
    kk = k[...]
    vv = v[...]
    for h in range(nheads):
        cols = slice(h * H, (h + 1) * H)
        st = jnp.where(allowed, nt(kk, q[:, cols]), -1e30)
        m = jnp.max(st, axis=0, keepdims=True)
        e = jnp.exp2((st - m) * (scale * math.log2(math.e)))
        p = e * (1.0 / jnp.sum(e, axis=0, keepdims=True))
        pt[:, cols] = p.astype(BF16)
        gp = nt(vv, g[:, cols])
        delta = jnp.sum(p * gp, axis=0, keepdims=True)
        dst[:, cols] = (p * (gp - delta)).astype(BF16)

    def stacked(ref):
        return jnp.concatenate([ref[:, h * H : (h + 1) * H] for h in range(nheads)], axis=0)

    gk = jnp.dot(dst[...], stacked(q), preferred_element_type=F32) * scale
    both[:, :H] = gk.astype(BF16)
    gv = jnp.dot(pt[...], stacked(g), preferred_element_type=F32)
    both[:, H:] = gv.astype(BF16)

    loads[4].wait()
    gkb = both[:, :H]

    @pl.loop(0, 16)
    def _(i):
        lanes = pl.ds(pl.multiple_of(i * 256, 256), 256)
        res = tn(xn[:, lanes], gkb)
        for n in range(8):
            place = n + c * (i % 8 - n)
            slot = i + c * ((i // 8) * 8 + n - i)
            wf[place, slot] = res[n * 32 : (n + 1) * 32]

    pl.semaphore_wait(barrier, len(peers))

    LO, HI = slice(0, 8), slice(8, 16)
    msgs = (mp_, mm_)
    recs = (rp, rm)

    def acopy(d, s, half):
        sl = pl.ds(half * 8, 8)
        return pltpu.make_async_remote_copy(
            src_ref=msgs[d].at[s, sl],
            dst_ref=recs[d].at[s, sl],
            send_sem=xs.at[d, s, half],
            recv_sem=xr.at[d, s, half],
            device_id=along_a(1 - 2 * d),
            device_id_type=MESH,
        )

    acopies = {}

    def asend(d, s, half, merged):
        sl = slice(half * 8, half * 8 + 8)
        target = (a + (1 - 2 * d) * (4 - s) + 8) % 8
        val = wf[target, sl]
        if merged:
            acopies[d, s - 1, half].wait_recv()
            val = val + recs[d][s - 1, sl].astype(F32)
        msgs[d][s, sl] = val.astype(BF16)
        cp = acopy(d, s, half)
        acopies[d, s, half] = cp
        cp.start()

    for d in range(2):
        asend(d, 0, d, False)
    for d in range(2):
        asend(d, 1, 1 - d, False)

    loads[5].wait()
    bb = both[...]

    def partial(yt, core):
        rows = pl.ds(pl.multiple_of((yt * 2 + core) * 512, 512), 512)
        return nt(bb[:, :H], pr[0, rows, :]) + nt(bb[:, H:], pr[1, rows, :])

    ccopies = []
    for n, dy in enumerate((2, 1, 3, 0)):
        bps[n] = partial((yh + dy) % 4, 1 - c).astype(BF16)
        cp = pltpu.make_async_remote_copy(
            src_ref=bps.at[n], dst_ref=bpr.at[n],
            send_sem=cs.at[n], recv_sem=cr.at[n],
            device_id=partner, device_id_type=MESH,
        )
        cp.start()
        ccopies.append(cp)
    for n, dy in enumerate((2, 1, 3, 0)):
        bpo[n] = partial((yh + dy) % 4, c)

    ysrc = (ysend_p, ysend_m)
    yrec = (yr_p, yr_m)
    ycopies = {}

    def ysend(d, piece):
        cp = pltpu.make_async_remote_copy(
            src_ref=ysrc[d].at[piece], dst_ref=yrec[d].at[piece],
            send_sem=ys.at[d, piece], recv_sem=yr.at[d, piece],
            device_id=along_y(1 - 2 * d), device_id_type=MESH,
        )
        ycopies[d, piece] = cp
        cp.start()

    def rows_of(d):
        return slice(d * 64, d * 64 + 64)

    ccopies[0].wait_recv()
    for d in range(2):
        r = rows_of(d)
        ysrc[d][0] = (bpo[0, r] + bpr[0, r].astype(F32)).astype(BF16)
        ysend(d, 0)
    for d in range(2):
        ccopies[1 + d].wait_recv()
        r = rows_of(1 - d)
        ysrc[d][1] = (bpo[1 + d, r] + bpr[1 + d, r].astype(F32)).astype(BF16)
        ysend(d, 1)

    for d in range(2):
        asend(d, 1, d, True)
    for d in range(2):
        asend(d, 2, 1 - d, True)

    def grad_query(hs):
        for h in hs:
            cols = slice(h * H, (h + 1) * H)
            gq[:, cols] = (tn(dst[:, cols], kk) * scale).astype(BF16)

    grad_query(range(0, 4))

    for d in range(2):
        asend(d, 2, d, True)
    for d in range(2):
        asend(d, 3, 1 - d, True)

    for d in range(2):
        ycopies[d, 0].wait_recv()
        r = rows_of(d)
        ysrc[d][2] = (
            bpo[1 + d, r] + bpr[1 + d, r].astype(F32) + yrec[d][0].astype(F32)
        ).astype(BF16)
        ysend(d, 2)

    grad_query(range(4, nheads))
    gq_out = pltpu.make_async_copy(gq, gq_hbm, osem)
    gq_out.start()

    for d in range(2):
        asend(d, 3, d, True)

    for d in range(2):
        for half in range(2):
            acopies[d, 3, half].wait_recv()
    tot = wf[a] + rp[3].astype(F32) + rm[3].astype(F32)
    wf[a] = tot
    s2[...] = tot.astype(BF16)
    b = z + c * (x - z)
    bcopies = []
    for n in range(15, 0, -1):
        slot = ((yl + n // 8) % 2) * 8 + (b + n % 8) % 8
        cp = pltpu.make_async_remote_copy(
            src_ref=s2.at[slot], dst_ref=r2.at[n],
            send_sem=s2s.at[n], recv_sem=s2r.at[n],
            device_id=along_b(n % 8, n // 8), device_id_type=MESH,
        )
        cp.start()
        bcopies.append(cp)

    ccopies[3].wait_recv()
    for d in range(2):
        for piece in (1, 2):
            ycopies[d, piece].wait_recv()
    for r in range(2):
        rr = rows_of(r)
        acc = bpo[3, rr] + bpr[3, rr].astype(F32)
        for d in range(2):
            acc = acc + yrec[d][2 if r == d else 1].astype(F32)
        gi_ref[rr, :] = acc.astype(BF16)

    own = wf[a, yl * 8 + b]
    for cp in bcopies:
        cp.wait_recv()
    for n in range(1, 16):
        own = own + r2[n].astype(F32)
    gw_ref[...] = own * (1.0 / (2 * 8 * 8))

    for cp in list(acopies.values()) + ccopies + list(ycopies.values()) + bcopies:
        cp.wait_send()
    gq_out.wait()


def body(query_states, key_states, value_states, grad_context, inputs_normed, projections):
    t, qw = query_states.shape
    d = inputs_normed.shape[1]
    hbm = pl.BlockSpec(memory_space=pl.ANY)
    vmem = pl.BlockSpec(memory_space=pltpu.VMEM)
    V = pltpu.VMEM
    S = pltpu.SemaphoreType.DMA
    gq, gi, gw = pl.pallas_call(
        kernel,
        out_shape=(
            jax.ShapeDtypeStruct((t, qw), BF16),
            jax.ShapeDtypeStruct((t, d // 8), BF16),
            jax.ShapeDtypeStruct((d // 128, H), F32),
        ),
        in_specs=[hbm] * 6,
        out_specs=(hbm, vmem, vmem),
        scratch_shapes=[
            V((t, qw), BF16), V((t, H), BF16), V((t, H), BF16), V((t, qw), BF16),
            V((t, d), BF16), V((2, d, H), BF16),
            V((t, qw), BF16), V((t, qw), BF16), V((t, qw), BF16), V((t, 2 * H), BF16),
            V((8, 16, 32, H), F32),
            V((4, 16, 32, H), BF16), V((4, 16, 32, H), BF16),
            V((4, 16, 32, H), BF16), V((4, 16, 32, H), BF16),
            V((16, 32, H), BF16), V((16, 32, H), BF16),
            V((4, t, 512), F32), V((4, t, 512), BF16), V((4, t, 512), BF16),
            V((3, t // 2, 512), BF16), V((3, t // 2, 512), BF16),
            V((3, t // 2, 512), BF16), V((3, t // 2, 512), BF16),
            S((6,)), S(()),
            S((2, 4, 2)), S((2, 4, 2)),
            S((16,)), S((16,)),
            S((4,)), S((4,)),
            S((2, 3)), S((2, 3)),
        ],
        compiler_params=pltpu.CompilerParams(collective_id=0, has_side_effects=True),
    )(query_states, key_states, value_states, grad_context, inputs_normed, projections)
    return gq, gi, gw


def solution(mesh):
    torus = Mesh(mesh.devices.reshape(2, 8, 8, 4, 2), DP + MP)
    return jax.shard_map(
        body,
        mesh=torus,
        in_specs=(P(DP, MP), P(DP, MP), P(DP, MP), P(DP, MP), P(DP, None), P(None, None, MP)),
        out_specs=(P(DP, MP), P(DP, MP), P(DP, MP)),
        check_vma=False,
    )
```

time: 157 us -> 49 us (0.31)
  the two profiles are of different devices: /device:TPU:1 before, /device:TPU:32 now
where the time goes in v1:
time: 49 us; the launch traced here: 48.7 us
  Pallas kernels  43.5 us (89%)
  local copies, waits for them, and re-layouts  4.56 us (9%)
  between operations  0.64 us (1%)
    pallas_call x1, Pallas kernels, body(): pl.pallas_call(kernel, out_shape=(jax.ShapeDtypeStruct((t, qw), BF16), ja...  43.5 us
    unnamed x3, local copies, waits for them, and re-layouts  4.56 us

profile of v1, /device:TPU:32, one launch (start us, length us, event | category | flops | bytes accessed | tf_op | source)
XLA Modules:
  0.0 48.7 jit_solution(17615331380663342764)
XLA Ops:
  0.6 43.5 %shard_map.85 = (bf16[128,1024]{1,0:T(8,128)(2,1)}, bf16[128,512]{1,0:T(8,128)(2,1)}, f32[32,128]{1,0:T(8,128)}) custom-call(bf16[128,1024]{1,0:T(8,128)(2,1)} %q_hbm.1, bf16[128,128]{1,0:T(8,128)(2,1)} %k_hbm.1, bf16[128,128]{1,0:T(8,128)(2,1)} %v_hbm.1, bf16[128,1024]{1,0:T(8,128)(2,1)} %g_hbm.1, bf16[128,4096]{1,0:T(8,128)(2,1)} %xn_hbm.1, ...), custom_call_target="tpu_custom_call" | custom-call | tf_op jit(solution)/shard_map/pallas_call | solution.py:275
  44.2 1.7 %copy.12 = bf16[128,1024]{1,0:T(8,128)(2,1)} copy(bf16[128,1024]{1,0:T(8,128)(2,1)} %get-tuple-element.6) | data formatting | bytes 524288
  45.8 1.6 %copy.13 = bf16[128,512]{1,0:T(8,128)(2,1)} copy(bf16[128,512]{1,0:T(8,128)(2,1)} %get-tuple-element.7) | data formatting | bytes 262144
  47.4 1.3 %copy.14 = f32[32,128]{1,0:T(8,128)} copy(f32[32,128]{1,0:T(8,128)} %get-tuple-element.8) | data formatting | bytes 32768

commit v2 on v1

v2 whole, which is shorter than its diff:
```python
import math

import jax
import jax.numpy as jnp
from jax import lax
from jax.experimental import pallas as pl
from jax.experimental.pallas import tpu as pltpu
from jax.sharding import Mesh
from jax.sharding import PartitionSpec as P

MESH = pl.DeviceIdType.MESH
H = 128
DP = ("yl", "z", "x")
MP = ("yh", "c")
F32 = jnp.float32
BF16 = jnp.bfloat16


def nt(a, b):
    return lax.dot_general(a, b, (((1,), (1,)), ((), ())), preferred_element_type=F32)


def tn(a, b):
    return lax.dot_general(a, b, (((0,), (0,)), ((), ())), preferred_element_type=F32)


NCH = 4


def toward(p, q):
    return 0 if q < p or (p == q and q >= 2) else 1


def merges(p, q):
    before = p - 1 if toward(p, q) == 0 else p + 1
    return 0 <= before <= 3 and toward(before, q) == toward(p, q)


def kernel(
    q_hbm, k_hbm, v_hbm, g_hbm, xn_hbm, pr_hbm,
    gq_out, gi_out, gw_out,
    q, k, v, g, xn, pr, pt, dst, gkt, both,
    wt, am, ar, xr, bm, br, fin, s2, r2,
    bpo, bps, bpr, ysend_p, ysend_m, yr_p, yr_m,
    lsem, as_, ars, xrs, bs, brs, s2s, s2r, cs, cr, ys, yr,
):
    yl = lax.axis_index("yl")
    z = lax.axis_index("z")
    x = lax.axis_index("x")
    yh = lax.axis_index("yh")
    c = lax.axis_index("c")
    nheads = q.shape[1] // H
    scale = 1.0 / math.sqrt(H)

    loads = [
        pltpu.make_async_copy(src, dst_, lsem.at[n])
        for n, (src, dst_) in enumerate(
            [(k_hbm, k), (q_hbm, q), (v_hbm, v), (g_hbm, g), (xn_hbm, xn), (pr_hbm, pr)]
        )
    ]
    for cp in loads[:5]:
        cp.start()

    def along_y(step):
        return {"yh": (yh + step + 4) % 4}

    def along_x(n):
        return {"x": (x + n % 8) % 8, "yl": (yl + n // 8) % 2}

    partner = {"c": 1 - c}
    peers = [partner, along_y(1), along_y(-1)]
    peers += [{"z": (z + n) % 8} for n in range(1, 8)]
    peers += [along_x(n) for n in range(1, 16)]
    barrier = pltpu.get_barrier_semaphore()
    for peer in peers:
        pl.semaphore_signal(barrier, inc=1, device_id=peer, device_id_type=MESH)

    def remote(src, dst_, ssem, rsem, device):
        return pltpu.make_async_remote_copy(
            src_ref=src, dst_ref=dst_, send_sem=ssem, recv_sem=rsem,
            device_id=device, device_id_type=MESH,
        )

    jpos = lax.broadcasted_iota(jnp.int32, (H, H), 0)
    ipos = lax.broadcasted_iota(jnp.int32, (H, H), 1)
    allowed = jpos <= ipos
    for n in range(4):
        loads[n].wait()
    loads[5].start()
    kk = k[...]
    vv = v[...]
    for h in range(nheads):
        cols = slice(h * H, (h + 1) * H)
        st = jnp.where(allowed, nt(kk, q[:, cols]), -1e30)
        m = jnp.max(st, axis=0, keepdims=True)
        e = jnp.exp2((st - m) * (scale * math.log2(math.e)))
        p = e * (1.0 / jnp.sum(e, axis=0, keepdims=True))
        pt[:, cols] = p.astype(BF16)
        gp = nt(vv, g[:, cols])
        delta = jnp.sum(p * gp, axis=0, keepdims=True)
        dst[:, cols] = (p * (gp - delta)).astype(BF16)

    def stacked(ref):
        return jnp.concatenate([ref[:, h * H : (h + 1) * H] for h in range(nheads)], axis=0)

    gk = jnp.dot(dst[...], stacked(q), preferred_element_type=F32) * scale
    both[:, :H] = gk.astype(BF16)
    gkt[...] = gk.T.astype(BF16)

    loads[4].wait()
    for t in range(8):
        for half in range(2):
            lanes = slice((half * 8 + t) * 256, (half * 8 + t + 1) * 256)
            wt[t, half] = jnp.dot(gkt[...], xn[:, lanes], preferred_element_type=F32)

    def partials():
        gv = jnp.dot(pt[...], stacked(g), preferred_element_type=F32)
        both[:, H:] = gv.astype(BF16)
        loads[5].wait()
        bb = both[...]

        def partial(yt, core):
            rows = pl.ds(pl.multiple_of((yt * 2 + core) * 512, 512), 512)
            return nt(bb[:, :H], pr[0, rows, :]) + nt(bb[:, H:], pr[1, rows, :])

        for n, dy in enumerate((2, 1, 3, 0)):
            bps[n] = partial((yh + dy) % 4, 1 - c).astype(BF16)
        for n, dy in enumerate((2, 1, 3, 0)):
            bpo[n] = partial((yh + dy) % 4, c)

    def grad_query():
        for h in range(nheads):
            cols = slice(h * H, (h + 1) * H)
            gq_out[:, cols] = (tn(dst[:, cols], kk) * scale).astype(BF16)

    ccopies = [remote(bps.at[n], bpr.at[n], cs.at[n], cr.at[n], partner) for n in range(4)]

    ysrc = (ysend_p, ysend_m)
    yrec = (yr_p, yr_m)
    ycopies = {
        (d, n): remote(ysrc[d].at[n], yrec[d].at[n], ys.at[d, n], yr.at[d, n], along_y(1 - 2 * d))
        for d in range(2)
        for n in range(3)
    }

    def rows_of(d):
        return slice(d * 64, d * 64 + 64)

    def y_swap():
        for cp in ccopies:
            cp.start()

    def y_first():
        ccopies[0].wait_recv()
        for d in range(2):
            r = rows_of(d)
            ysrc[d][0] = (bpo[0, r] + bpr[0, r].astype(F32)).astype(BF16)
            ycopies[d, 0].start()
        for d in range(2):
            ccopies[1 + d].wait_recv()
            r = rows_of(1 - d)
            ysrc[d][1] = (bpo[1 + d, r] + bpr[1 + d, r].astype(F32)).astype(BF16)
            ycopies[d, 1].start()

    def y_second():
        for d in range(2):
            ycopies[d, 0].wait_recv()
            r = rows_of(d)
            ysrc[d][2] = (
                bpo[1 + d, r] + bpr[1 + d, r].astype(F32) + yrec[d][0].astype(F32)
            ).astype(BF16)
            ycopies[d, 2].start()

    def piece(ch):
        return ch // 2, pl.ds(ch % 2 * 64, 64)

    def across(hf, p, qs):
        for q_ in qs:
            d = toward(p, q_)
            last = p == (3 if d == 0 else 0)
            t = 4 * (1 - hf) + q_
            for ch in range(NCH):
                half, rows = piece(ch)
                val = wt[t, half, rows]
                if merges(p, q_):
                    here = ar.at[q_, half, rows]
                    remote(am.at[q_, half, rows], here, as_.at[q_, ch], ars.at[q_, ch], {"z": t}).wait_recv()
                    val = val + ar[q_, half, rows].astype(F32)
                am[q_, half, rows] = val.astype(BF16)
                if last:
                    to, sem, dev = xr.at[d, half, rows], xrs.at[d, ch], t
                else:
                    to, sem, dev = ar.at[q_, half, rows], ars.at[q_, ch], 4 * hf + p + 1 - 2 * d
                remote(am.at[q_, half, rows], to, as_.at[q_, ch], sem, {"z": dev}).start()

    def waits_late(p, q_):
        return toward(p, q_) == 1 and merges(p, q_)

    def within_target(n):
        return z // 4 * 4 + (z % 4 + n) % 4

    bcopies = [
        remote(bm.at[n - 1], br.at[n - 1], bs.at[n - 1], brs.at[n - 1], {"z": within_target(n)})
        for n in range(1, 4)
    ]

    def within():
        for n in range(1, 4):
            bm[n - 1] = wt[within_target(n)].astype(BF16)
            bcopies[n - 1].start()

    @pl.when(z < 4)
    def _():
        partials()
        grad_query()

    pl.semaphore_wait(barrier, len(peers))

    @pl.when(z < 4)
    def _():
        y_swap()
        within()
        for p in range(4):
            pl.when(z == p)(lambda p=p: across(0, p, [n for n in range(4) if not waits_late(p, n)]))
        y_first()
        for p in range(2):
            pl.when(z == p)(lambda p=p: across(0, p, [n for n in range(4) if waits_late(p, n)]))
        y_second()

    @pl.when(z >= 4)
    def _():
        for p in range(4):
            pl.when(z == 4 + p)(lambda p=p: across(1, p, range(4)))
        within()
        partials()
        y_swap()
        grad_query()
        y_first()
        y_second()

    for cp in bcopies:
        cp.wait_recv()
    for d in range(2):
        for ch in range(NCH):
            half, rows = piece(ch)
            remote(
                am.at[0, half, rows], xr.at[d, half, rows], as_.at[0, ch], xrs.at[d, ch], {"z": (z + 1) % 8}
            ).wait_recv()
    for half in range(2):
        tot = wt[z, half] + xr[0, half].astype(F32) + xr[1, half].astype(F32)
        for n in range(3):
            tot = tot + br[n, half].astype(F32)
        tot = tot.T.reshape(8, 32, H)
        fin[half * 8 : half * 8 + 8] = tot
        s2[half * 8 : half * 8 + 8] = tot.astype(BF16)
    scopies = []
    for n in (4, 12, 3, 5, 11, 13, 2, 6, 10, 14, 1, 7, 9, 15, 8):
        slot = (yl + n // 8) % 2 * 8 + (x + n % 8) % 8
        cp = remote(s2.at[slot], r2.at[n], s2s.at[n], s2r.at[n], along_x(n))
        cp.start()
        scopies.append(cp)

    ccopies[3].wait_recv()
    for d in range(2):
        for n in (1, 2):
            ycopies[d, n].wait_recv()
    for r in range(2):
        rr = rows_of(r)
        acc = bpo[3, rr] + bpr[3, rr].astype(F32)
        for d in range(2):
            acc = acc + yrec[d][2 if r == d else 1].astype(F32)
        gi_out[rr, :] = acc.astype(BF16)

    own = fin[yl * 8 + x]
    for cp in scopies:
        cp.wait_recv()
    for n in range(1, 16):
        own = own + r2[n].astype(F32)
    gw_out[...] = own * (1.0 / (2 * 8 * 8))

    for cp in ccopies + list(ycopies.values()) + bcopies + scopies:
        cp.wait_send()
    for q_ in range(4):
        for ch in range(NCH):
            half, rows = piece(ch)
            remote(
                am.at[q_, half, rows], ar.at[q_, half, rows], as_.at[q_, ch], ars.at[q_, ch], {"z": (z + 1) % 8}
            ).wait_send()


def put_out(*refs):
    n = len(refs) // 2
    sem = refs[-1]
    copies = [
        pltpu.make_async_copy(src, dst_, sem.at[i])
        for i, (src, dst_) in enumerate(zip(refs[:n], refs[n : 2 * n]))
    ]
    for cp in copies:
        cp.start()
    for cp in copies:
        cp.wait()


def body(query_states, key_states, value_states, grad_context, inputs_normed, projections):
    t, qw = query_states.shape
    d = inputs_normed.shape[1]
    hbm = pl.BlockSpec(memory_space=pl.ANY)
    vmem = pl.BlockSpec(memory_space=pltpu.VMEM)
    V = pltpu.VMEM
    S = pltpu.SemaphoreType.DMA
    shapes = (
        jax.ShapeDtypeStruct((t, qw), BF16),
        jax.ShapeDtypeStruct((t, d // 8), BF16),
        jax.ShapeDtypeStruct((d // 128, H), F32),
    )
    outs = pl.pallas_call(
        kernel,
        out_shape=tuple(V(s.shape, s.dtype) for s in shapes),
        in_specs=[hbm] * 6,
        out_specs=(vmem,) * 3,
        scratch_shapes=[
            V((t, qw), BF16), V((t, H), BF16), V((t, H), BF16), V((t, qw), BF16),
            V((t, d), BF16), V((2, d, H), BF16),
            V((t, qw), BF16), V((t, qw), BF16), V((H, t), BF16), V((t, 2 * H), BF16),
            V((8, 2, H, 256), F32),
            V((4, 2, H, 256), BF16), V((4, 2, H, 256), BF16), V((2, 2, H, 256), BF16),
            V((3, 2, H, 256), BF16), V((3, 2, H, 256), BF16),
            V((16, 32, H), F32), V((16, 32, H), BF16), V((16, 32, H), BF16),
            V((4, t, 512), F32), V((4, t, 512), BF16), V((4, t, 512), BF16),
            V((3, t // 2, 512), BF16), V((3, t // 2, 512), BF16),
            V((3, t // 2, 512), BF16), V((3, t // 2, 512), BF16),
            S((6,)), S((4, NCH)), S((4, NCH)), S((2, NCH)), S((3,)), S((3,)),
            S((16,)), S((16,)), S((4,)), S((4,)), S((2, 3)), S((2, 3)),
        ],
        compiler_params=pltpu.CompilerParams(collective_id=0, has_side_effects=True),
    )(query_states, key_states, value_states, grad_context, inputs_normed, projections)
    return pl.pallas_call(
        put_out,
        out_shape=shapes,
        in_specs=(vmem,) * 3,
        out_specs=(hbm,) * 3,
        scratch_shapes=[S((3,))],
    )(*[pltpu.with_memory_space_constraint(o, pltpu.VMEM) for o in outs])


def solution(mesh):
    torus = Mesh(mesh.devices.reshape(2, 8, 8, 4, 2), DP + MP)
    return jax.shard_map(
        body,
        mesh=torus,
        in_specs=(P(DP, MP), P(DP, MP), P(DP, MP), P(DP, MP), P(DP, None), P(None, None, MP)),
        out_specs=(P(DP, MP), P(DP, MP), P(DP, MP)),
        check_vma=False,
    )
```

time: 49 us -> 56.3 us (1.15)
  the two profiles are of different devices: /device:TPU:32 before, /device:TPU:496 now
where the time goes in v2:
time: 56.3 us; the launch traced here: 56.2 us
  Pallas kernels  55.5 us (99%)
  between operations  0.64 us (1%)
    pallas_call x1, Pallas kernels, body(): pl.pallas_call(kernel, out_shape=tuple((V(s.shape, s.dtype) for s in shap...  54.7 us

profile of v2, /device:TPU:496, one launch (start us, length us, event | category | flops | bytes accessed | tf_op | source)
XLA Modules:
  0.0 56.2 jit_solution(2233395111629646794)
XLA Ops:
  0.6 54.7 %shard_map.85 = (bf16[128,1024]{1,0:T(8,128)(2,1)S(1)}, bf16[128,512]{1,0:T(8,128)(2,1)S(1)}, f32[32,128]{1,0:T(8,128)S(1)}) custom-call(bf16[128,1024]{1,0:T(8,128)(2,1)} %q_hbm.1, bf16[128,128]{1,0:T(8,128)(2,1)} %k_hbm.1, bf16[128,128]{1,0:T(8,128)(2,1)} %v_hbm.1, bf16[128,1024]{1,0:T(8,128)(2,1)} %g_hbm.1, bf16[128,4096]{1,0:T(8,128)(2,1)} %xn_hbm.1, ...), custom_call_target="tpu_custom_call" | custom-call | tf_op jit(solution)/shard_map/pallas_call | solution.py:316
  55.4 0.8 %shard_map.86 = (bf16[128,1024]{1,0:T(8,128)(2,1)}, bf16[128,512]{1,0:T(8,128)(2,1)}, f32[32,128]{1,0:T(8,128)}) custom-call(bf16[128,1024]{1,0:T(8,128)(2,1)S(1)} %get-tuple-element.6.refs_0_, bf16[128,512]{1,0:T(8,128)(2,1)S(1)} %get-tuple-element.7.refs_1_, f32[32,128]{1,0:T(8,128)S(1)} %get-tuple-element.8.refs_2_), custom_call_target="tpu_custom_call" | custom-call | tf_op jit(solution)/shard_map/pallas_call | solution.py:337

commit v3 on v2

--- a/solution.py
+++ b/solution.py
@@ -27,22 +27,27 @@
 NCH = 4
 
 
-def toward(p, q):
-    return 0 if q < p or (p == q and q >= 2) else 1
-
-
-def merges(p, q):
-    before = p - 1 if toward(p, q) == 0 else p + 1
-    return 0 <= before <= 3 and toward(before, q) == toward(p, q)
+def swap_pieces(tiles):
+    lane = lax.broadcasted_iota(jnp.int32, tiles[0].shape, 1)
+    for far, width in ((2, 64), (1, 32)):
+        low = lane // width % 2 == 0
+        out = list(tiles)
+        for i in range(4):
+            if i // far % 2 == 0:
+                p, q = tiles[i], tiles[i + far]
+                out[i] = jnp.where(low, p, pltpu.roll(q, width, 1))
+                out[i + far] = jnp.where(low, pltpu.roll(p, H - width, 1), q)
+        tiles = out
+    return tiles
 
 
 def kernel(
     q_hbm, k_hbm, v_hbm, g_hbm, xn_hbm, pr_hbm,
     gq_out, gi_out, gw_out,
-    q, k, v, g, xn, pr, pt, dst, gkt, both,
-    wt, am, ar, xr, bm, br, fin, s2, r2,
+    q, k, v, g, xn, xp, pr, pt, dst, gkt, both,
+    wt, am, ar, fm, fr, fin, s2, r2,
     bpo, bps, bpr, ysend_p, ysend_m, yr_p, yr_m,
-    lsem, as_, ars, xrs, bs, brs, s2s, s2r, cs, cr, ys, yr,
+    lsem, as_, ars, fs, frs, s2s, s2r, cs, cr, ys, yr,
 ):
     yl = lax.axis_index("yl")
     z = lax.axis_index("z")
@@ -64,13 +69,19 @@
     def along_y(step):
         return {"yh": (yh + step + 4) % 4}
 
-    def along_x(n):
-        return {"x": (x + n % 8) % 8, "yl": (yl + n // 8) % 2}
+    a = x + c * (z - x)
+    b = z + c * (x - z)
+
+    def along_a(step):
+        return {"x": (x + (1 - c) * step + 8) % 8, "z": (z + c * step + 8) % 8}
+
+    def along_b(n):
+        return {"x": (x + c * (n % 8)) % 8, "z": (z + (1 - c) * (n % 8)) % 8, "yl": (yl + n // 8) % 2}
 
     partner = {"c": 1 - c}
     peers = [partner, along_y(1), along_y(-1)]
-    peers += [{"z": (z + n) % 8} for n in range(1, 8)]
-    peers += [along_x(n) for n in range(1, 16)]
+    peers += [along_a(n) for n in (1, -1, 3, -3)]
+    peers += [along_b(n) for n in range(1, 16)]
     barrier = pltpu.get_barrier_semaphore()
     for peer in peers:
         pl.semaphore_signal(barrier, inc=1, device_id=peer, device_id_type=MESH)
@@ -108,10 +119,27 @@
     gkt[...] = gk.T.astype(BF16)
 
     loads[4].wait()
+
+    @pl.when(c == 0)
+    def _():
+        for zq in range(4):
+            for xh in range(2):
+                cols = [((zq * 4 + zr) * 2 + xh) * H for zr in range(4)]
+                tiles = swap_pieces([xn[:, i : i + H] for i in cols])
+                for xl in range(4):
+                    to = ((xh * 4 + xl) * 4 + zq) * H
+                    xp[:, to : to + H] = tiles[xl]
+
+    @pl.when(c == 1)
+    def _():
+        for half in range(2):
+            for t in range(8):
+                xp[:, (t * 2 + half) * 256 : (t * 2 + half + 1) * 256] = xn[
+                    :, (half * 8 + t) * 256 : (half * 8 + t + 1) * 256
+                ]
+
     for t in range(8):
-        for half in range(2):
-            lanes = slice((half * 8 + t) * 256, (half * 8 + t + 1) * 256)
-            wt[t, half] = jnp.dot(gkt[...], xn[:, lanes], preferred_element_type=F32)
+        wt[t] = jnp.dot(gkt[...], xp[:, t * 512 : (t + 1) * 512], preferred_element_type=F32)
 
     def partials():
         gv = jnp.dot(pt[...], stacked(g), preferred_element_type=F32)
@@ -171,43 +199,62 @@
             ).astype(BF16)
             ycopies[d, 2].start()
 
-    def piece(ch):
-        return ch // 2, pl.ds(ch % 2 * 64, 64)
-
-    def across(hf, p, qs):
-        for q_ in qs:
-            d = toward(p, q_)
-            last = p == (3 if d == 0 else 0)
-            t = 4 * (1 - hf) + q_
+    acopies = {
+        (d, m, ch): remote(
+            am.at[d, m, pl.ds(ch * 32, 32)], ar.at[d, m, pl.ds(ch * 32, 32)],
+            as_.at[d, m, ch], ars.at[d, m, ch], along_a(1 - 2 * d),
+        )
+        for d in range(2)
+        for m in range(3)
+        for ch in range(NCH)
+    }
+    fcopies = [remote(fm.at[d], fr.at[d], fs.at[d], frs.at[d], along_a(3 - 6 * d)) for d in range(2)]
+
+    def chunks(d):
+        return (2, 3, 0, 1) if d == 0 else (0, 1, 2, 3)
+
+    def ring(m, d, ch):
+        rows = slice(ch * 32, ch * 32 + 32)
+        val = wt[(a + (1 - 2 * d) * (3 - m) + 8) % 8, rows]
+        if m:
+            acopies[d, m - 1, ch].wait_recv()
+            val = val + ar[d, m - 1, rows].astype(F32)
+        if m == 2 and ch // 2 == d:
+            if ch % 2 == 0:
+                fcopies[d].wait_recv()
+            val = val + fr[d, ch % 2 * 32 : ch % 2 * 32 + 32].astype(F32)
+        am[d, m, rows] = val.astype(BF16)
+        acopies[d, m, ch].start()
+
+    def ring_step(m):
+        for i in range(NCH):
+            for d in range(2):
+                ring(m, d, chunks(d)[i])
+
+    def ring_start():
+        ring_step(0)
+        for d in range(2):
+            fm[d] = wt[(a + 4) % 8, d * 64 : d * 64 + 64].astype(BF16)
+            fcopies[d].start()
+
+    slots = (4, 12, 3, 5, 11, 13, 2, 6, 10, 14, 1, 7, 9, 15, 8)
+    scopies = [
+        remote(s2.at[(yl + n // 8) % 2 * 8 + (b + n % 8) % 8], r2.at[n], s2s.at[n], s2r.at[n], along_b(n))
+        for n in slots
+    ]
+
+    def owners():
+        for d in range(2):
             for ch in range(NCH):
-                half, rows = piece(ch)
-                val = wt[t, half, rows]
-                if merges(p, q_):
-                    here = ar.at[q_, half, rows]
-                    remote(am.at[q_, half, rows], here, as_.at[q_, ch], ars.at[q_, ch], {"z": t}).wait_recv()
-                    val = val + ar[q_, half, rows].astype(F32)
-                am[q_, half, rows] = val.astype(BF16)
-                if last:
-                    to, sem, dev = xr.at[d, half, rows], xrs.at[d, ch], t
-                else:
-                    to, sem, dev = ar.at[q_, half, rows], ars.at[q_, ch], 4 * hf + p + 1 - 2 * d
-                remote(am.at[q_, half, rows], to, as_.at[q_, ch], sem, {"z": dev}).start()
-
-    def waits_late(p, q_):
-        return toward(p, q_) == 1 and merges(p, q_)
-
-    def within_target(n):
-        return z // 4 * 4 + (z % 4 + n) % 4
-
-    bcopies = [
-        remote(bm.at[n - 1], br.at[n - 1], bs.at[n - 1], brs.at[n - 1], {"z": within_target(n)})
-        for n in range(1, 4)
-    ]
-
-    def within():
-        for n in range(1, 4):
-            bm[n - 1] = wt[within_target(n)].astype(BF16)
-            bcopies[n - 1].start()
+                acopies[d, 2, ch].wait_recv()
+        for half in range(2):
+            cols = slice(half * 256, half * 256 + 256)
+            tot = wt[a, :, cols] + ar[0, 2, :, cols].astype(F32) + ar[1, 2, :, cols].astype(F32)
+            tot = tot.T.reshape(8, 32, H)
+            fin[half * 8 : half * 8 + 8] = tot
+            s2[half * 8 : half * 8 + 8] = tot.astype(BF16)
+        for cp in scopies:
+            cp.start()
 
     @pl.when(z < 4)
     def _():
@@ -215,50 +262,27 @@
         grad_query()
 
     pl.semaphore_wait(barrier, len(peers))
+    ring_start()
 
     @pl.when(z < 4)
     def _():
         y_swap()
-        within()
-        for p in range(4):
-            pl.when(z == p)(lambda p=p: across(0, p, [n for n in range(4) if not waits_late(p, n)]))
         y_first()
-        for p in range(2):
-            pl.when(z == p)(lambda p=p: across(0, p, [n for n in range(4) if waits_late(p, n)]))
+        ring_step(1)
         y_second()
+        ring_step(2)
+        owners()
 
     @pl.when(z >= 4)
     def _():
-        for p in range(4):
-            pl.when(z == 4 + p)(lambda p=p: across(1, p, range(4)))
-        within()
+        ring_step(1)
+        ring_step(2)
+        owners()
         partials()
         y_swap()
         grad_query()
         y_first()
         y_second()
-
-    for cp in bcopies:
-        cp.wait_recv()
-    for d in range(2):
-        for ch in range(NCH):
-            half, rows = piece(ch)
-            remote(
-                am.at[0, half, rows], xr.at[d, half, rows], as_.at[0, ch], xrs.at[d, ch], {"z": (z + 1) % 8}
-            ).wait_recv()
-    for half in range(2):
-        tot = wt[z, half] + xr[0, half].astype(F32) + xr[1, half].astype(F32)
-        for n in range(3):
-            tot = tot + br[n, half].astype(F32)
-        tot = tot.T.reshape(8, 32, H)
-        fin[half * 8 : half * 8 + 8] = tot
-        s2[half * 8 : half * 8 + 8] = tot.astype(BF16)
-    scopies = []
-    for n in (4, 12, 3, 5, 11, 13, 2, 6, 10, 14, 1, 7, 9, 15, 8):
-        slot = (yl + n // 8) % 2 * 8 + (x + n % 8) % 8
-        cp = remote(s2.at[slot], r2.at[n], s2s.at[n], s2r.at[n], along_x(n))
-        cp.start()
-        scopies.append(cp)
 
     ccopies[3].wait_recv()
     for d in range(2):
@@ -271,21 +295,15 @@
             acc = acc + yrec[d][2 if r == d else 1].astype(F32)
         gi_out[rr, :] = acc.astype(BF16)
 
-    own = fin[yl * 8 + x]
+    own = fin[yl * 8 + b]
     for cp in scopies:
         cp.wait_recv()
     for n in range(1, 16):
         own = own + r2[n].astype(F32)
     gw_out[...] = own * (1.0 / (2 * 8 * 8))
 
-    for cp in ccopies + list(ycopies.values()) + bcopies + scopies:
+    for cp in ccopies + list(ycopies.values()) + list(acopies.values()) + fcopies + scopies:
         cp.wait_send()
-    for q_ in range(4):
-        for ch in range(NCH):
-            half, rows = piece(ch)
-            remote(
-                am.at[q_, half, rows], ar.at[q_, half, rows], as_.at[q_, ch], ars.at[q_, ch], {"z": (z + 1) % 8}
-            ).wait_send()
 
 
 def put_out(*refs):
@@ -320,16 +338,16 @@
         out_specs=(vmem,) * 3,
         scratch_shapes=[
             V((t, qw), BF16), V((t, H), BF16), V((t, H), BF16), V((t, qw), BF16),
-            V((t, d), BF16), V((2, d, H), BF16),
+            V((t, d), BF16), V((t, d), BF16), V((2, d, H), BF16),
             V((t, qw), BF16), V((t, qw), BF16), V((H, t), BF16), V((t, 2 * H), BF16),
-            V((8, 2, H, 256), F32),
-            V((4, 2, H, 256), BF16), V((4, 2, H, 256), BF16), V((2, 2, H, 256), BF16),
-            V((3, 2, H, 256), BF16), V((3, 2, H, 256), BF16),
+            V((8, H, 512), F32),
+            V((2, 3, H, 512), BF16), V((2, 3, H, 512), BF16),
+            V((2, H // 2, 512), BF16), V((2, H // 2, 512), BF16),
             V((16, 32, H), F32), V((16, 32, H), BF16), V((16, 32, H), BF16),
             V((4, t, 512), F32), V((4, t, 512), BF16), V((4, t, 512), BF16),
             V((3, t // 2, 512), BF16), V((3, t // 2, 512), BF16),
             V((3, t // 2, 512), BF16), V((3, t // 2, 512), BF16),
-            S((6,)), S((4, NCH)), S((4, NCH)), S((2, NCH)), S((3,)), S((3,)),
+            S((6,)), S((2, 3, NCH)), S((2, 3, NCH)), S((2,)), S((2,)),
             S((16,)), S((16,)), S((4,)), S((4,)), S((2, 3)), S((2, 3)),
         ],
         compiler_params=pltpu.CompilerParams(collective_id=0, has_side_effects=True),

time: 56.3 us -> 43.1 us (0.77)
  the two profiles are of different devices: /device:TPU:496 before, /device:TPU:1 now
where the time goes in v3:
time: 43.1 us; the launch traced here: 42.9 us
  Pallas kernels  42.3 us (98%)
  between operations  0.64 us (1%)
    pallas_call x1, Pallas kernels, body(): pl.pallas_call(kernel, out_shape=tuple((V(s.shape, s.dtype) for s in shap...  41.5 us

profile of v3, /device:TPU:1, one launch (start us, length us, event | category | flops | bytes accessed | tf_op | source)
XLA Modules:
  0.0 42.9 jit_solution(16087588565502094565)
XLA Ops:
  0.6 41.5 %shard_map.85 = (bf16[128,1024]{1,0:T(8,128)(2,1)S(1)}, bf16[128,512]{1,0:T(8,128)(2,1)S(1)}, f32[32,128]{1,0:T(8,128)S(1)}) custom-call(bf16[128,1024]{1,0:T(8,128)(2,1)} %q_hbm.1, bf16[128,128]{1,0:T(8,128)(2,1)} %k_hbm.1, bf16[128,128]{1,0:T(8,128)(2,1)} %v_hbm.1, bf16[128,1024]{1,0:T(8,128)(2,1)} %g_hbm.1, bf16[128,4096]{1,0:T(8,128)(2,1)} %xn_hbm.1, ...), custom_call_target="tpu_custom_call" | custom-call | tf_op jit(solution)/shard_map/pallas_call | solution.py:334
  42.2 0.8 %shard_map.86 = (bf16[128,1024]{1,0:T(8,128)(2,1)}, bf16[128,512]{1,0:T(8,128)(2,1)}, f32[32,128]{1,0:T(8,128)}) custom-call(bf16[128,1024]{1,0:T(8,128)(2,1)S(1)} %get-tuple-element.6.refs_0_, bf16[128,512]{1,0:T(8,128)(2,1)S(1)} %get-tuple-element.7.refs_1_, f32[32,128]{1,0:T(8,128)S(1)} %get-tuple-element.8.refs_2_), custom_call_target="tpu_custom_call" | custom-call | tf_op jit(solution)/shard_map/pallas_call | solution.py:355

commit v4 on v3

--- a/solution.py
+++ b/solution.py
@@ -28,17 +28,15 @@
 
 
 def swap_pieces(tiles):
-    lane = lax.broadcasted_iota(jnp.int32, tiles[0].shape, 1)
-    for far, width in ((2, 64), (1, 32)):
-        low = lane // width % 2 == 0
-        out = list(tiles)
-        for i in range(4):
-            if i // far % 2 == 0:
-                p, q = tiles[i], tiles[i + far]
-                out[i] = jnp.where(low, p, pltpu.roll(q, width, 1))
-                out[i + far] = jnp.where(low, pltpu.roll(p, H - width, 1), q)
-        tiles = out
-    return tiles
+    place = lax.broadcasted_iota(jnp.int32, tiles[0].shape, 1) // 32
+    turned = [tiles[0]] + [pltpu.roll(tiles[j], 32 * j, 1) for j in range(1, 4)]
+    out = []
+    for i in range(4):
+        mixed = turned[0]
+        for j in range(1, 4):
+            mixed = jnp.where(place == (i + j) % 4, turned[j], mixed)
+        out.append(pltpu.roll(mixed, H - 32 * i, 1) if i else mixed)
+    return out
 
 
 def kernel(
@@ -138,8 +136,11 @@
                     :, (half * 8 + t) * 256 : (half * 8 + t + 1) * 256
                 ]
 
-    for t in range(8):
-        wt[t] = jnp.dot(gkt[...], xp[:, t * 512 : (t + 1) * 512], preferred_element_type=F32)
+    def weight_terms(t):
+        lanes = pl.ds(pl.multiple_of(t * 512, 512), 512)
+        res = jnp.dot(gkt[...], xp[:, lanes], preferred_element_type=F32)
+        for ch in range(NCH):
+            wt[t, ch] = res[:, ch * H : ch * H + H]
 
     def partials():
         gv = jnp.dot(pt[...], stacked(g), preferred_element_type=F32)
@@ -199,62 +200,63 @@
             ).astype(BF16)
             ycopies[d, 2].start()
 
-    acopies = {
-        (d, m, ch): remote(
-            am.at[d, m, pl.ds(ch * 32, 32)], ar.at[d, m, pl.ds(ch * 32, 32)],
-            as_.at[d, m, ch], ars.at[d, m, ch], along_a(1 - 2 * d),
+    def acopy(d, m, ch):
+        return remote(
+            am.at[d, m, ch], ar.at[d, m, ch], as_.at[d, m, ch], ars.at[d, m, ch], along_a(1 - 2 * d)
         )
-        for d in range(2)
-        for m in range(3)
-        for ch in range(NCH)
-    }
-    fcopies = [remote(fm.at[d], fr.at[d], fs.at[d], frs.at[d], along_a(3 - 6 * d)) for d in range(2)]
-
-    def chunks(d):
-        return (2, 3, 0, 1) if d == 0 else (0, 1, 2, 3)
-
-    def ring(m, d, ch):
-        rows = slice(ch * 32, ch * 32 + 32)
-        val = wt[(a + (1 - 2 * d) * (3 - m) + 8) % 8, rows]
-        if m:
-            acopies[d, m - 1, ch].wait_recv()
-            val = val + ar[d, m - 1, rows].astype(F32)
-        if m == 2 and ch // 2 == d:
-            if ch % 2 == 0:
-                fcopies[d].wait_recv()
-            val = val + fr[d, ch % 2 * 32 : ch % 2 * 32 + 32].astype(F32)
-        am[d, m, rows] = val.astype(BF16)
-        acopies[d, m, ch].start()
+
+    def fcopy(d):
+        return remote(fm.at[d], fr.at[d], fs.at[d], frs.at[d], along_a(3 - 6 * d))
+
+    def ring(m, d):
+        for ch in range(NCH):
+            val = wt[(a + (1 - 2 * d) * (3 - m) + 8) % 8, ch]
+            if m:
+                acopy(d, m - 1, ch).wait_recv()
+                val = val + ar[d, m - 1, ch].astype(F32)
+            am[d, m, ch] = val.astype(BF16)
+            if m == 2:
+                @pl.when(d == ch // 2)
+                def _():
+                    if ch % 2 == 0:
+                        fcopy(ch // 2).wait_recv()
+                    am[ch // 2, m, ch] = (val + fr[ch // 2, ch % 2].astype(F32)).astype(BF16)
+
+            acopy(d, m, ch).start()
+
+    low = (7 - a) // 4
 
     def ring_step(m):
-        for i in range(NCH):
+        ring(m, low)
+        ring(m, 1 - low)
+
+    def ring_start():
+        for step in (3, 5):
+            weight_terms((a + step) % 8)
+        ring_step(0)
+        weight_terms((a + 4) % 8)
+        for d in range(2):
+            fm[d] = wt[(a + 4) % 8, 2 * d : 2 * d + 2].astype(BF16)
+            fcopy(d).start()
+        for step in (2, 6, 1, 7, 0):
+            weight_terms((a + step) % 8)
+
+    mine = yl * 8 + b
+
+    def scopy(slot):
+        n = (slot // 8 - yl + 2) % 2 * 8 + (slot % 8 - b + 8) % 8
+        return remote(s2.at[slot], r2.at[n], s2s.at[slot], s2r.at[n], along_b(n))
+
+    def owners():
+        for ch in range(NCH):
             for d in range(2):
-                ring(m, d, chunks(d)[i])
-
-    def ring_start():
-        ring_step(0)
-        for d in range(2):
-            fm[d] = wt[(a + 4) % 8, d * 64 : d * 64 + 64].astype(BF16)
-            fcopies[d].start()
-
-    slots = (4, 12, 3, 5, 11, 13, 2, 6, 10, 14, 1, 7, 9, 15, 8)
-    scopies = [
-        remote(s2.at[(yl + n // 8) % 2 * 8 + (b + n % 8) % 8], r2.at[n], s2s.at[n], s2r.at[n], along_b(n))
-        for n in slots
-    ]
-
-    def owners():
-        for d in range(2):
-            for ch in range(NCH):
-                acopies[d, 2, ch].wait_recv()
-        for half in range(2):
-            cols = slice(half * 256, half * 256 + 256)
-            tot = wt[a, :, cols] + ar[0, 2, :, cols].astype(F32) + ar[1, 2, :, cols].astype(F32)
-            tot = tot.T.reshape(8, 32, H)
-            fin[half * 8 : half * 8 + 8] = tot
-            s2[half * 8 : half * 8 + 8] = tot.astype(BF16)
-        for cp in scopies:
-            cp.start()
+                acopy(d, 2, ch).wait_recv()
+            tot = wt[a, ch] + ar[0, 2, ch].astype(F32) + ar[1, 2, ch].astype(F32)
+            tot = tot.T.reshape(4, 32, H)
+            fin[ch * 4 : ch * 4 + 4] = tot
+            s2[ch * 4 : ch * 4 + 4] = tot.astype(BF16)
+            for slot in range(ch * 4, ch * 4 + 4):
+                pl.when(mine != slot)(lambda slot=slot: scopy(slot).start())
 
     @pl.when(z < 4)
     def _():
@@ -269,19 +271,19 @@
         y_swap()
         y_first()
         ring_step(1)
+        ring_step(2)
         y_second()
-        ring_step(2)
         owners()
 
     @pl.when(z >= 4)
     def _():
+        partials()
+        y_swap()
         ring_step(1)
         ring_step(2)
+        y_first()
         owners()
-        partials()
-        y_swap()
         grad_query()
-        y_first()
         y_second()
 
     ccopies[3].wait_recv()
@@ -295,15 +297,22 @@
             acc = acc + yrec[d][2 if r == d else 1].astype(F32)
         gi_out[rr, :] = acc.astype(BF16)
 
-    own = fin[yl * 8 + b]
-    for cp in scopies:
-        cp.wait_recv()
+    own = fin[mine]
+    for n in range(1, 16):
+        remote(s2.at[0], r2.at[n], s2s.at[0], s2r.at[n], along_b(n)).wait_recv()
     for n in range(1, 16):
         own = own + r2[n].astype(F32)
     gw_out[...] = own * (1.0 / (2 * 8 * 8))
 
-    for cp in ccopies + list(ycopies.values()) + list(acopies.values()) + fcopies + scopies:
+    for cp in ccopies + list(ycopies.values()):
         cp.wait_send()
+    for d in range(2):
+        fcopy(d).wait_send()
+        for m in range(3):
+            for ch in range(NCH):
+                acopy(d, m, ch).wait_send()
+    for slot in range(16):
+        pl.when(mine != slot)(lambda slot=slot: scopy(slot).wait_send())
 
 
 def put_out(*refs):
@@ -340,9 +349,9 @@
             V((t, qw), BF16), V((t, H), BF16), V((t, H), BF16), V((t, qw), BF16),
             V((t, d), BF16), V((t, d), BF16), V((2, d, H), BF16),
             V((t, qw), BF16), V((t, qw), BF16), V((H, t), BF16), V((t, 2 * H), BF16),
-            V((8, H, 512), F32),
-            V((2, 3, H, 512), BF16), V((2, 3, H, 512), BF16),
-            V((2, H // 2, 512), BF16), V((2, H // 2, 512), BF16),
+            V((8, NCH, H, H), F32),
+            V((2, 3, NCH, H, H), BF16), V((2, 3, NCH, H, H), BF16),
+            V((2, 2, H, H), BF16), V((2, 2, H, H), BF16),
             V((16, 32, H), F32), V((16, 32, H), BF16), V((16, 32, H), BF16),
             V((4, t, 512), F32), V((4, t, 512), BF16), V((4, t, 512), BF16),
             V((3, t // 2, 512), BF16), V((3, t // 2, 512), BF16),

time: 43.1 us -> 41.3 us (0.958)
  the two profiles are of different devices: /device:TPU:1 before, /device:TPU:80 now
where the time goes in v4:
time: 41.3 us; the launch traced here: 41.1 us
  Pallas kernels  40.5 us (98%)
  between operations  0.64 us (2%)
    pallas_call x1, Pallas kernels, body(): pl.pallas_call(kernel, out_shape=tuple((V(s.shape, s.dtype) for s in shap...  39.7 us

profile of v4, /device:TPU:80, one launch (start us, length us, event | category | flops | bytes accessed | tf_op | source)
XLA Modules:
  0.0 41.1 jit_solution(13311828226620641350)
XLA Ops:
  0.6 39.7 %shard_map.85 = (bf16[128,1024]{1,0:T(8,128)(2,1)S(1)}, bf16[128,512]{1,0:T(8,128)(2,1)S(1)}, f32[32,128]{1,0:T(8,128)S(1)}) custom-call(bf16[128,1024]{1,0:T(8,128)(2,1)} %q_hbm.1, bf16[128,128]{1,0:T(8,128)(2,1)} %k_hbm.1, bf16[128,128]{1,0:T(8,128)(2,1)} %v_hbm.1, bf16[128,1024]{1,0:T(8,128)(2,1)} %g_hbm.1, bf16[128,4096]{1,0:T(8,128)(2,1)} %xn_hbm.1, ...), custom_call_target="tpu_custom_call" | custom-call | tf_op jit(solution)/shard_map/pallas_call | solution.py:343
  40.4 0.8 %shard_map.86 = (bf16[128,1024]{1,0:T(8,128)(2,1)}, bf16[128,512]{1,0:T(8,128)(2,1)}, f32[32,128]{1,0:T(8,128)}) custom-call(bf16[128,1024]{1,0:T(8,128)(2,1)S(1)} %get-tuple-element.6.refs_0_, bf16[128,512]{1,0:T(8,128)(2,1)S(1)} %get-tuple-element.7.refs_1_, f32[32,128]{1,0:T(8,128)S(1)} %get-tuple-element.8.refs_2_), custom_call_target="tpu_custom_call" | custom-call | tf_op jit(solution)/shard_map/pallas_call | solution.py:364

commit v5 on v4

--- a/solution.py
+++ b/solution.py
@@ -25,6 +25,7 @@
 
 
 NCH = 4
+EARLY = 2
 
 
 def swap_pieces(tiles):
@@ -44,8 +45,9 @@
     gq_out, gi_out, gw_out,
     q, k, v, g, xn, xp, pr, pt, dst, gkt, both,
     wt, am, ar, fm, fr, fin, s2, r2,
+    we, em, er, efm, ef, s2e, own_,
     bpo, bps, bpr, ysend_p, ysend_m, yr_p, yr_m,
-    lsem, as_, ars, fs, frs, s2s, s2r, cs, cr, ys, yr,
+    lsem, as_, ars, fs, frs, es, ers, efs, efr, s2es, s2s, s2r, cs, cr, ys, yr,
 ):
     yl = lax.axis_index("yl")
     z = lax.axis_index("z")
@@ -78,8 +80,8 @@
 
     partner = {"c": 1 - c}
     peers = [partner, along_y(1), along_y(-1)]
-    peers += [along_a(n) for n in (1, -1, 3, -3)]
     peers += [along_b(n) for n in range(1, 16)]
+    peers += [{**along_a(n % 8), "yl": (yl + n // 8) % 2} for n in range(1, 16) if n != 8]
     barrier = pltpu.get_barrier_semaphore()
     for peer in peers:
         pl.semaphore_signal(barrier, inc=1, device_id=peer, device_id_type=MESH)
@@ -116,25 +118,24 @@
     both[:, :H] = gk.astype(BF16)
     gkt[...] = gk.T.astype(BF16)
 
-    loads[4].wait()
-
-    @pl.when(c == 0)
-    def _():
-        for zq in range(4):
-            for xh in range(2):
-                cols = [((zq * 4 + zr) * 2 + xh) * H for zr in range(4)]
-                tiles = swap_pieces([xn[:, i : i + H] for i in cols])
-                for xl in range(4):
-                    to = ((xh * 4 + xl) * 4 + zq) * H
-                    xp[:, to : to + H] = tiles[xl]
-
-    @pl.when(c == 1)
-    def _():
-        for half in range(2):
-            for t in range(8):
-                xp[:, (t * 2 + half) * 256 : (t * 2 + half + 1) * 256] = xn[
-                    :, (half * 8 + t) * 256 : (half * 8 + t + 1) * 256
-                ]
+    def permute():
+        @pl.when(c == 0)
+        def _():
+            for zq in range(4):
+                for xh in range(2):
+                    cols = [((zq * 4 + zr) * 2 + xh) * H for zr in range(4)]
+                    tiles = swap_pieces([xn[:, i : i + H] for i in cols])
+                    for xl in range(4):
+                        to = ((xh * 4 + xl) * 4 + zq) * H
+                        xp[:, to : to + H] = tiles[xl]
+
+        @pl.when(c == 1)
+        def _():
+            for half in range(2):
+                for t in range(8):
+                    xp[:, (t * 2 + half) * 256 : (t * 2 + half + 1) * 256] = xn[
+                        :, (half * 8 + t) * 256 : (half * 8 + t + 1) * 256
+                    ]
 
     def weight_terms(t):
         lanes = pl.ds(pl.multiple_of(t * 512, 512), 512)
@@ -241,11 +242,87 @@
         for step in (2, 6, 1, 7, 0):
             weight_terms((a + step) % 8)
 
+    def early_terms():
+        for t in range(EARLY):
+            for half in range(2):
+                lanes = slice((half * 8 + t) * 256, (half * 8 + t + 1) * 256)
+                res = jnp.dot(gkt[...], xn[:, lanes], preferred_element_type=F32)
+                for xh in range(2):
+                    we[t, half * 2 + xh] = res[:, xh * H : xh * H + H]
+
+    def at(t, r):
+        return jnp.logical_and(c == 0, (z - t + 8) % 8 == r)
+
+    def ecopy(t, r, ch):
+        d = 1 if r < 4 else 0
+        return remote(
+            em.at[t, ch], er.at[t, d, ch], es.at[t, ch], ers.at[t, d, ch], {"z": (z + 1 - 2 * d + 8) % 8}
+        )
+
+    def efcopy(t, d):
+        return remote(efm.at[t, d], ef.at[t], efs.at[t, d], efr.at[t], {"z": (z + 3 - 6 * d + 8) % 8})
+
+    def early_far(t):
+        for d in range(2):
+            efm[t, d] = we[t, 2 * d : 2 * d + 2].astype(BF16)
+            efcopy(t, d).start()
+
+    def early_chain(t, r):
+        d = 1 if r < 4 else 0
+        for ch in range(NCH):
+            val = we[t, ch]
+            if r not in (3, 5):
+                ecopy(t, r, ch).wait_recv()
+                val = val + er[t, d, ch].astype(F32)
+            if r in (1, 7) and ch // 2 == d:
+                if ch % 2 == 0:
+                    efcopy(t, d).wait_recv()
+                val = val + ef[t, ch % 2].astype(F32)
+            em[t, ch] = val.astype(BF16)
+            ecopy(t, r, ch).start()
+
+    def early(*rs):
+        for t in range(EARLY):
+            for r in rs:
+                if r == 4:
+                    pl.when(at(t, r))(lambda t=t: early_far(t))
+                else:
+                    pl.when(at(t, r))(lambda t=t, r=r: early_chain(t, r))
+
+    def escopy(slot):
+        n = (slot // 8 - yl + 2) % 2 * 8 + (slot % 8 - x + 8) % 8
+        return remote(
+            s2e.at[slot], r2.at[n], s2es.at[slot], s2r.at[n], {"x": (x + n % 8) % 8, "yl": (yl + n // 8) % 2}
+        )
+
+    own_early = jnp.logical_and(c == 0, z < EARLY)
+
+    def early_owner(t):
+        for ch in range(NCH):
+            for d in range(2):
+                ecopy(t, 1 if d else 7, ch).wait_recv()
+            tot = we[t, ch] + er[t, 0, ch].astype(F32) + er[t, 1, ch].astype(F32)
+            tot = tot.T.reshape(4, 32, H)
+            s2e[ch * 4 : ch * 4 + 4] = tot.astype(BF16)
+            for i in range(4):
+                slot = ch * 4 + i
+                pl.when(yl * 8 + x == slot)(lambda tot=tot, i=i: own_.__setitem__(..., tot[i]))
+                pl.when(yl * 8 + x != slot)(lambda slot=slot: escopy(slot).start())
+
+    def early_owners():
+        for t in range(EARLY):
+            pl.when(at(t, 0))(lambda t=t: early_owner(t))
+
     mine = yl * 8 + b
 
     def scopy(slot):
         n = (slot // 8 - yl + 2) % 2 * 8 + (slot % 8 - b + 8) % 8
         return remote(s2.at[slot], r2.at[n], s2s.at[slot], s2r.at[n], along_b(n))
+
+    def sends(slot):
+        if slot % 8 < EARLY:
+            return jnp.logical_and(c == 1, mine != slot)
+        return mine != slot
 
     def owners():
         for ch in range(NCH):
@@ -256,7 +333,10 @@
             fin[ch * 4 : ch * 4 + 4] = tot
             s2[ch * 4 : ch * 4 + 4] = tot.astype(BF16)
             for slot in range(ch * 4, ch * 4 + 4):
-                pl.when(mine != slot)(lambda slot=slot: scopy(slot).start())
+                pl.when(sends(slot))(lambda slot=slot: scopy(slot).start())
+
+    loads[4].wait()
+    pl.when(c == 0)(early_terms)
 
     @pl.when(z < 4)
     def _():
@@ -264,22 +344,30 @@
         grad_query()
 
     pl.semaphore_wait(barrier, len(peers))
+    early(5, 3, 4)
+    permute()
     ring_start()
 
     @pl.when(z < 4)
     def _():
         y_swap()
         y_first()
+        early(2)
         ring_step(1)
+        early(1)
         ring_step(2)
+        early(7)
         y_second()
         owners()
+        early_owners()
 
     @pl.when(z >= 4)
     def _():
+        early(6)
         partials()
         y_swap()
         ring_step(1)
+        early(7)
         ring_step(2)
         y_first()
         owners()
@@ -297,7 +385,11 @@
             acc = acc + yrec[d][2 if r == d else 1].astype(F32)
         gi_out[rr, :] = acc.astype(BF16)
 
-    own = fin[mine]
+    @pl.when(jnp.logical_not(own_early))
+    def _():
+        own_[...] = fin[mine]
+
+    own = own_[...]
     for n in range(1, 16):
         remote(s2.at[0], r2.at[n], s2s.at[0], s2r.at[n], along_b(n)).wait_recv()
     for n in range(1, 16):
@@ -312,7 +404,13 @@
             for ch in range(NCH):
                 acopy(d, m, ch).wait_send()
     for slot in range(16):
-        pl.when(mine != slot)(lambda slot=slot: scopy(slot).wait_send())
+        pl.when(sends(slot))(lambda slot=slot: scopy(slot).wait_send())
+        pl.when(jnp.logical_and(own_early, yl * 8 + x != slot))(lambda slot=slot: escopy(slot).wait_send())
+    for t in range(EARLY):
+        for ch in range(NCH):
+            pl.when(jnp.logical_and(c == 0, (z - t + 8) % 4 != 0))(lambda t=t, ch=ch: ecopy(t, 1, ch).wait_send())
+        for d in range(2):
+            pl.when(at(t, 4))(lambda t=t, d=d: efcopy(t, d).wait_send())
 
 
 def put_out(*refs):
@@ -353,10 +451,13 @@
             V((2, 3, NCH, H, H), BF16), V((2, 3, NCH, H, H), BF16),
             V((2, 2, H, H), BF16), V((2, 2, H, H), BF16),
             V((16, 32, H), F32), V((16, 32, H), BF16), V((16, 32, H), BF16),
+            V((EARLY, NCH, H, H), F32), V((EARLY, NCH, H, H), BF16), V((EARLY, 2, NCH, H, H), BF16),
+            V((EARLY, 2, 2, H, H), BF16), V((EARLY, 2, H, H), BF16), V((16, 32, H), BF16), V((32, H), F32),
             V((4, t, 512), F32), V((4, t, 512), BF16), V((4, t, 512), BF16),
             V((3, t // 2, 512), BF16), V((3, t // 2, 512), BF16),
             V((3, t // 2, 512), BF16), V((3, t // 2, 512), BF16),
             S((6,)), S((2, 3, NCH)), S((2, 3, NCH)), S((2,)), S((2,)),
+            S((EARLY, NCH)), S((EARLY, 2, NCH)), S((EARLY, 2)), S((EARLY,)), S((16,)),
             S((16,)), S((16,)), S((4,)), S((4,)), S((2, 3)), S((2, 3)),
         ],
         compiler_params=pltpu.CompilerParams(collective_id=0, has_side_effects=True),

time: 41.3 us -> 44 us (1.065)
  the two profiles are of different devices: /device:TPU:80 before, /device:TPU:146 now
where the time goes in v5:
time: 44 us; the launch traced here: 43.8 us
  Pallas kernels  43.1 us (98%)
  between operations  0.64 us (1%)
    pallas_call x1, Pallas kernels, body(): pl.pallas_call(kernel, out_shape=tuple((V(s.shape, s.dtype) for s in shap...  42.4 us

profile of v5, /device:TPU:146, one launch (start us, length us, event | category | flops | bytes accessed | tf_op | source)
XLA Modules:
  0.0 43.8 jit_solution(4682414295716335897)
XLA Ops:
  0.6 42.4 %shard_map.85 = (bf16[128,1024]{1,0:T(8,128)(2,1)S(1)}, bf16[128,512]{1,0:T(8,128)(2,1)S(1)}, f32[32,128]{1,0:T(8,128)S(1)}) custom-call(bf16[128,1024]{1,0:T(8,128)(2,1)} %q_hbm.1, bf16[128,128]{1,0:T(8,128)(2,1)} %k_hbm.1, bf16[128,128]{1,0:T(8,128)(2,1)} %v_hbm.1, bf16[128,1024]{1,0:T(8,128)(2,1)} %g_hbm.1, bf16[128,4096]{1,0:T(8,128)(2,1)} %xn_hbm.1, ...), custom_call_target="tpu_custom_call" | custom-call | tf_op jit(solution)/shard_map/pallas_call | solution.py:441
  43.0 0.8 %shard_map.86 = (bf16[128,1024]{1,0:T(8,128)(2,1)}, bf16[128,512]{1,0:T(8,128)(2,1)}, f32[32,128]{1,0:T(8,128)}) custom-call(bf16[128,1024]{1,0:T(8,128)(2,1)S(1)} %get-tuple-element.6.refs_0_, bf16[128,512]{1,0:T(8,128)(2,1)S(1)} %get-tuple-element.7.refs_1_, f32[32,128]{1,0:T(8,128)S(1)} %get-tuple-element.8.refs_2_), custom_call_target="tpu_custom_call" | custom-call | tf_op jit(solution)/shard_map/pallas_call | solution.py:465

commit v6 on v4

--- a/solution.py
+++ b/solution.py
@@ -205,11 +205,11 @@
             am.at[d, m, ch], ar.at[d, m, ch], as_.at[d, m, ch], ars.at[d, m, ch], along_a(1 - 2 * d)
         )
 
-    def fcopy(d):
-        return remote(fm.at[d], fr.at[d], fs.at[d], frs.at[d], along_a(3 - 6 * d))
-
-    def ring(m, d):
-        for ch in range(NCH):
+    def fcopy(d, i):
+        return remote(fm.at[d, i], fr.at[d, i], fs.at[d, i], frs.at[d, i], along_a(3 - 6 * d))
+
+    def ring(m, d, wave):
+        for ch in (wave, wave + 2):
             val = wt[(a + (1 - 2 * d) * (3 - m) + 8) % 8, ch]
             if m:
                 acopy(d, m - 1, ch).wait_recv()
@@ -218,28 +218,40 @@
             if m == 2:
                 @pl.when(d == ch // 2)
                 def _():
-                    if ch % 2 == 0:
-                        fcopy(ch // 2).wait_recv()
-                    am[ch // 2, m, ch] = (val + fr[ch // 2, ch % 2].astype(F32)).astype(BF16)
+                    fcopy(ch // 2, wave).wait_recv()
+                    am[ch // 2, m, ch] = (val + fr[ch // 2, wave].astype(F32)).astype(BF16)
 
             acopy(d, m, ch).start()
 
-    low = (7 - a) // 4
-
-    def ring_step(m):
-        ring(m, low)
-        ring(m, 1 - low)
+    low = c * ((7 - a) // 4) + (1 - c) * (a // 4)
+
+    def ring_step(m, wave):
+        ring(m, low, wave)
+        ring(m, 1 - low, wave)
+
+    def start_wave(wave):
+        ring_step(0, wave)
+        for d in range(2):
+            fm[d, wave] = wt[(a + 4) % 8, 2 * d + wave].astype(BF16)
+            fcopy(d, wave).start()
 
     def ring_start():
-        for step in (3, 5):
+        for step in (3, 5, 4):
             weight_terms((a + step) % 8)
-        ring_step(0)
-        weight_terms((a + 4) % 8)
-        for d in range(2):
-            fm[d] = wt[(a + 4) % 8, 2 * d : 2 * d + 2].astype(BF16)
-            fcopy(d).start()
+        start_wave(0)
         for step in (2, 6, 1, 7, 0):
             weight_terms((a + step) % 8)
+
+    def ring_middle():
+        ring_step(1, 0)
+        start_wave(1)
+        ring_step(2, 0)
+        ring_step(1, 1)
+
+    def ring_end():
+        owners(0)
+        ring_step(2, 1)
+        owners(1)
 
     mine = yl * 8 + b
 
@@ -247,8 +259,8 @@
         n = (slot // 8 - yl + 2) % 2 * 8 + (slot % 8 - b + 8) % 8
         return remote(s2.at[slot], r2.at[n], s2s.at[slot], s2r.at[n], along_b(n))
 
-    def owners():
-        for ch in range(NCH):
+    def owners(wave):
+        for ch in (wave, wave + 2):
             for d in range(2):
                 acopy(d, 2, ch).wait_recv()
             tot = wt[a, ch] + ar[0, 2, ch].astype(F32) + ar[1, 2, ch].astype(F32)
@@ -270,19 +282,29 @@
     def _():
         y_swap()
         y_first()
-        ring_step(1)
-        ring_step(2)
+        ring_middle()
         y_second()
-        owners()
-
-    @pl.when(z >= 4)
+        ring_end()
+
+    @pl.when(jnp.logical_and(z >= 4, z < 6))
     def _():
         partials()
         y_swap()
-        ring_step(1)
-        ring_step(2)
+        ring_middle()
         y_first()
-        owners()
+        ring_end()
+        grad_query()
+        y_second()
+
+    @pl.when(z >= 6)
+    def _():
+        ring_middle()
+        owners(0)
+        partials()
+        y_swap()
+        ring_step(2, 1)
+        owners(1)
+        y_first()
         grad_query()
         y_second()
 
@@ -307,7 +329,8 @@
     for cp in ccopies + list(ycopies.values()):
         cp.wait_send()
     for d in range(2):
-        fcopy(d).wait_send()
+        for i in range(2):
+            fcopy(d, i).wait_send()
         for m in range(3):
             for ch in range(NCH):
                 acopy(d, m, ch).wait_send()
@@ -356,7 +379,7 @@
             V((4, t, 512), F32), V((4, t, 512), BF16), V((4, t, 512), BF16),
             V((3, t // 2, 512), BF16), V((3, t // 2, 512), BF16),
             V((3, t // 2, 512), BF16), V((3, t // 2, 512), BF16),
-            S((6,)), S((2, 3, NCH)), S((2, 3, NCH)), S((2,)), S((2,)),
+            S((6,)), S((2, 3, NCH)), S((2, 3, NCH)), S((2, 2)), S((2, 2)),
             S((16,)), S((16,)), S((4,)), S((4,)), S((2, 3)), S((2, 3)),
         ],
         compiler_params=pltpu.CompilerParams(collective_id=0, has_side_effects=True),

time: 41.3 us -> 40.7 us (0.985)
  the two profiles are of different devices: /device:TPU:80 before, /device:TPU:14 now
where the time goes in v6:
time: 40.7 us; the launch traced here: 40.5 us
  Pallas kernels  39.9 us (98%)
  between operations  0.64 us (2%)
    pallas_call x1, Pallas kernels, body(): pl.pallas_call(kernel, out_shape=tuple((V(s.shape, s.dtype) for s in shap...  39.1 us

profile of v6, /device:TPU:14, one launch (start us, length us, event | category | flops | bytes accessed | tf_op | source)
XLA Modules:
  0.0 40.5 jit_solution(12073590084265593489)
XLA Ops:
  0.6 39.1 %shard_map.85 = (bf16[128,1024]{1,0:T(8,128)(2,1)S(1)}, bf16[128,512]{1,0:T(8,128)(2,1)S(1)}, f32[32,128]{1,0:T(8,128)S(1)}) custom-call(bf16[128,1024]{1,0:T(8,128)(2,1)} %q_hbm.1, bf16[128,128]{1,0:T(8,128)(2,1)} %k_hbm.1, bf16[128,128]{1,0:T(8,128)(2,1)} %v_hbm.1, bf16[128,1024]{1,0:T(8,128)(2,1)} %g_hbm.1, bf16[128,4096]{1,0:T(8,128)(2,1)} %xn_hbm.1, ...), custom_call_target="tpu_custom_call" | custom-call | tf_op jit(solution)/shard_map/pallas_call | solution.py:366
  39.8 0.8 %shard_map.86 = (bf16[128,1024]{1,0:T(8,128)(2,1)}, bf16[128,512]{1,0:T(8,128)(2,1)}, f32[32,128]{1,0:T(8,128)}) custom-call(bf16[128,1024]{1,0:T(8,128)(2,1)S(1)} %get-tuple-element.6.refs_0_, bf16[128,512]{1,0:T(8,128)(2,1)S(1)} %get-tuple-element.7.refs_1_, f32[32,128]{1,0:T(8,128)S(1)} %get-tuple-element.8.refs_2_), custom_call_target="tpu_custom_call" | custom-call | tf_op jit(solution)/shard_map/pallas_call | solution.py:387
